TPU v7x, 32 devices: a whole 2x2x4 slice. The times are simulated.
32 devices in a mesh: groups: 2 (over x), asset: 16 (over z, y, core).
Axes of the slice: x: 2, y: 2, z: 4, core: 2. Of those that a mesh axis runs over, the one named last changes fastest.
Arguments:
- scen_draws: bfloat16 [8192, 256], P(('groups', 'asset')), parts along dimension 0, may hold values from -4 to 4
- factor_mix: bfloat16 [256, 256], replicated, may hold values from -0.375 to 0.375
- loadings: bfloat16 [32768, 256], P(('groups', 'asset')), parts along dimension 0, may hold values from -0.375 to 0.375
- convexity: float32 [32768], P(('groups', 'asset')), parts along dimension 0, may hold values from -0.6 to 0.6
- holdings: float32 [32768], P(('groups', 'asset')), parts along dimension 0, may hold values from -0.22097087 to 0.22097087
- desk_map: int32 [32768], P(('groups', 'asset')), parts along dimension 0, may hold values from 0 to 127
- ranks: int32 [8192], P('groups'), parts along dimension 0, may hold values from 0 to 4095, each once
- desk_prices: float32 [256], P('groups'), parts along dimension 0, may hold values from -5 to 5
Outputs:
- allocation: float32 [256], P('groups'), parts along dimension 0
- grad_loadings: float32 [32768, 256], P(('groups', 'asset')), parts along dimension 0
- grad_convexity: float32 [32768], P(('groups', 'asset')), parts along dimension 0
There are 2 independent parts, one for each index of `groups`. A program takes and returns all parts, laid end to end along the dimension named above; an argument that names none is the same for every part. Nothing has to cross between parts.
All inputs are finite; a program needn't handle non-finite values.
Results may differ from a plain program's by a relative error of at most 0.0029.
Values may be sent and summed in bfloat16 or wider, within the bound.
A program may use at most 64 MiB of HBM per device.

v0:
```python
import math

import jax
import jax.numpy as jnp
from jax import lax
from jax.sharding import PartitionSpec as P

DESKS = 128
BAND = 32
CENTER = 166


def smooth_bend(value):
    return jnp.logaddexp(value, -value) - math.log(2.0)


def rank_kernel(ranks, scenarios):
    centre = jnp.float32(CENTER)
    spread = jnp.float32(BAND)
    offsets = (ranks.astype(jnp.float32) - centre) / spread
    every = (jnp.arange(scenarios, dtype=jnp.float32) - centre) / spread
    return jnp.exp(-0.5 * offsets * offsets) / jnp.sum(jnp.exp(-0.5 * every * every))


def cotangent_of(
    weights,
    weight_total,
    slopes,
    smoothing,
    kernel,
    grad_quant,
    grad_band,
    centred,
    prices,
    scenarios,
):
    grad_loss = (
        slopes / smoothing
        + kernel * grad_quant
        + grad_band * 0.09 * centred / (scenarios * smoothing)
    )
    return (
        scenarios * (-weights[:, None] * prices[None, :] / weight_total - grad_loss[:, None])
    ).astype(jnp.bfloat16)


def tail_core(losses, valued, ranks, prices):
    scenarios = losses.shape[0]
    kernel = rank_kernel(ranks, scenarios)
    quantile = jnp.sum(kernel * losses)
    average = jnp.mean(losses)
    centred = losses - average
    smoothing = 0.3 * jnp.sqrt(jnp.mean(centred * centred) + 1e-06)
    scores = (losses - quantile) / smoothing
    weights = jax.nn.sigmoid(scores)
    weight_total = jnp.sum(weights)
    objective = -jnp.sum(weights * valued) / weight_total
    slopes = (-valued - objective) / weight_total * weights * (1.0 - weights)
    grad_quant = -jnp.sum(slopes) / smoothing
    grad_band = -jnp.sum(slopes * scores) / smoothing
    cotangent = cotangent_of(
        weights,
        weight_total,
        slopes,
        smoothing,
        kernel,
        grad_quant,
        grad_band,
        centred,
        prices,
        scenarios,
    )
    return (cotangent, weights, weight_total)


def tail_terms(desk_pnl, ranks, prices):
    losses = -jnp.sum(desk_pnl, axis=1)
    valued = jnp.sum(desk_pnl * prices[None, :], axis=1)
    cotangent, weights, weight_total = tail_core(losses, valued, ranks, prices)
    allocation = -jnp.sum(weights[:, None] * desk_pnl, axis=0) / weight_total
    return (cotangent, allocation)


def desk_table(desk_map):
    columns = jnp.arange(DESKS, dtype=jnp.int32)
    return (desk_map[:, None] == columns[None, :]).astype(jnp.bfloat16)


def split_rows(array, block_rows):
    return array.reshape((-1, block_rows) + array.shape[1:])


def exposure_of(shock_rows, loadings):
    return lax.dot_general(
        shock_rows, loadings, (((1,), (1,)), ((), ())), preferred_element_type=jnp.float32
    )


def pnl_rows(shock_rows, loadings, convexity, holdings, table):
    number = shock_rows.shape[0]
    block_rows = math.gcd(number, 512)

    def pnl_one_block(shock_block):
        exposure = exposure_of(shock_block, loadings)
        held = (holdings * (exposure + convexity * smooth_bend(exposure))).astype(jnp.bfloat16)
        return jnp.dot(held, table, preferred_element_type=jnp.float32)

    result = lax.map(pnl_one_block, split_rows(shock_rows, block_rows))
    return result.reshape((number, table.shape[1]))


def grad_rows(carry, shock_rows, cot_rows, loadings, convexity, holdings, table):
    number = shock_rows.shape[0]
    block_rows = math.gcd(number, 512)

    def grad_one_block(state, inputs):
        shock_block, cot_block = inputs
        exposure = exposure_of(shock_block, loadings)
        spread_back = lax.dot_general(
            cot_block, table, (((1,), (1,)), ((), ())), preferred_element_type=jnp.float32
        )
        held = holdings * spread_back
        grad_exposure = (held * (1.0 + convexity * jnp.tanh(exposure))).astype(jnp.bfloat16)
        grad_load = state[0] + lax.dot_general(
            grad_exposure, shock_block, (((0,), (0,)), ((), ())), preferred_element_type=jnp.float32
        )
        grad_conv = state[1] + jnp.sum(held * smooth_bend(exposure), axis=0)
        return ((grad_load, grad_conv), None)

    final, ignored = lax.scan(
        grad_one_block,
        carry,
        (split_rows(shock_rows, block_rows), split_rows(cot_rows, block_rows)),
    )
    return final


def shards(scen_draws, factor_mix, loadings, convexity, holdings, desk_map, ranks, desk_prices):
    local_shocks = jnp.dot(scen_draws, factor_mix, preferred_element_type=jnp.float32).astype(
        jnp.bfloat16
    )
    table = desk_table(desk_map)
    shocks = lax.all_gather(local_shocks, "asset", axis=0, tiled=True)
    partial_value = pnl_rows(shocks, loadings, convexity, holdings, table)
    desk_pnl = lax.psum(partial_value, "asset")
    cotangent, allocation = tail_terms(desk_pnl, ranks, desk_prices)
    initial = (
        jnp.zeros((loadings.shape[0], loadings.shape[1]), jnp.float32),
        jnp.zeros((loadings.shape[0],), jnp.float32),
    )
    grad_load, grad_conv = grad_rows(
        initial, shocks, cotangent, loadings, convexity, holdings, table
    )
    squares = lax.psum(jnp.sum(grad_load * grad_load) + jnp.sum(grad_conv * grad_conv), "asset")
    entries = loadings.shape[0] * lax.axis_size("asset") * (loadings.shape[1] + 1)
    factor = lax.rsqrt(squares / entries + 1e-06)
    return (allocation, grad_load * factor, grad_conv * factor)


def solution(mesh):
    placed = (
        P(("groups", "asset"), None),
        P(),
        P(("groups", "asset"), None),
        P(("groups", "asset")),
        P(("groups", "asset")),
        P(("groups", "asset")),
        P("groups"),
        P("groups"),
    )
    return jax.shard_map(
        shards,
        mesh=mesh,
        in_specs=placed,
        out_specs=(P("groups"), P(("groups", "asset"), None), P(("groups", "asset"))),
        check_vma=False,
    )
```

profile of v0, /device:TPU:0, one launch (start us, length us, event | category | flops | bytes accessed | tf_op | source)
XLA Modules:
  0.0 288.6 jit_solution(887370904575663468)
XLA Ops:
  9.9 45.0 %all-gather.2.cloned.1.call-done = bf16[4096,256]{1,0:T(8,128)(2,1)} async-done(((bf16[256,256]{1,0:T(8,128)(2,1)}), bf16[4096,256]{1,0:T(8,128)(2,1)}) %all-gather.2.cloned.1.call-update) | async-done | bytes 2097168 | tf_op jit(solution)/shard_map/all_gather | solution.py:143
  54.9 30.3 %while.28 = (s32[]{:T(128)}, f32[8,512,128]{2,1,0:T(8,128)}, f32[1024]{0:T(1024)}, bf16[8,512,256]{2,1,0:T(8,128)(2,1)}, bf16[1024,256]{1,0:T(8,128)(2,1)}, /*index=5*/f32[1024]{0:T(1024)}, s32[1024]{0:T(1024)}, s32[]{:T(128)}) while((s32[]{:T(128)}, f32[8,512,128]{2,1,0:T(8,128)}, f32[1024]{0:T(1024)}, ...), condition=%wide.region_1.2_spmd.clone, body=%wide.region_0.1_spmd.clone.sunk | while | flops 410255360 | bytes 1061981 | solution.py:108
  54.9 3.8 %fusion.70 = f32[8,512,128]{2,1,0:T(8,128)} fusion(f32[8,512,128]{2,1,0:T(8,128)} %get-tuple-element.417, s32[]{:T(128)S(6)} %copy.14, bf16[1024,256]{1,0:T(8,128)(2,1)} %get-tuple-element.428, f32[1024]{0:T(1024)} %get-tuple-element.429, f32[1024]{0:T(1024)} %get-tuple-element.426, s32[1024]{0:T(1024)} %get-tuple-element.430, ...), kind=kOutput, calls=%fused_computation.14.clone.1 | convolution fusion | flops 410255360 | bytes 1061888 | tf_op jit(solution)/shard_map/while/body/eval_jaxpr/dot_general | solution.py:106
  58.7 3.8 %fusion.70 = f32[8,512,128]{2,1,0:T(8,128)} fusion(f32[8,512,128]{2,1,0:T(8,128)} %get-tuple-element.417, s32[]{:T(128)S(6)} %copy.14, bf16[1024,256]{1,0:T(8,128)(2,1)} %get-tuple-element.428, f32[1024]{0:T(1024)} %get-tuple-element.429, f32[1024]{0:T(1024)} %get-tuple-element.426, s32[1024]{0:T(1024)} %get-tuple-element.430, ...), kind=kOutput, calls=%fused_computation.14.clone.1 | convolution fusion | flops 410255360 | bytes 1061888 | tf_op jit(solution)/shard_map/while/body/eval_jaxpr/dot_general | solution.py:106
  62.5 3.8 %fusion.70 = f32[8,512,128]{2,1,0:T(8,128)} fusion(f32[8,512,128]{2,1,0:T(8,128)} %get-tuple-element.417, s32[]{:T(128)S(6)} %copy.14, bf16[1024,256]{1,0:T(8,128)(2,1)} %get-tuple-element.428, f32[1024]{0:T(1024)} %get-tuple-element.429, f32[1024]{0:T(1024)} %get-tuple-element.426, s32[1024]{0:T(1024)} %get-tuple-element.430, ...), kind=kOutput, calls=%fused_computation.14.clone.1 | convolution fusion | flops 410255360 | bytes 1061888 | tf_op jit(solution)/shard_map/while/body/eval_jaxpr/dot_general | solution.py:106
  66.3 3.8 %fusion.70 = f32[8,512,128]{2,1,0:T(8,128)} fusion(f32[8,512,128]{2,1,0:T(8,128)} %get-tuple-element.417, s32[]{:T(128)S(6)} %copy.14, bf16[1024,256]{1,0:T(8,128)(2,1)} %get-tuple-element.428, f32[1024]{0:T(1024)} %get-tuple-element.429, f32[1024]{0:T(1024)} %get-tuple-element.426, s32[1024]{0:T(1024)} %get-tuple-element.430, ...), kind=kOutput, calls=%fused_computation.14.clone.1 | convolution fusion | flops 410255360 | bytes 1061888 | tf_op jit(solution)/shard_map/while/body/eval_jaxpr/dot_general | solution.py:106
  70.1 3.8 %fusion.70 = f32[8,512,128]{2,1,0:T(8,128)} fusion(f32[8,512,128]{2,1,0:T(8,128)} %get-tuple-element.417, s32[]{:T(128)S(6)} %copy.14, bf16[1024,256]{1,0:T(8,128)(2,1)} %get-tuple-element.428, f32[1024]{0:T(1024)} %get-tuple-element.429, f32[1024]{0:T(1024)} %get-tuple-element.426, s32[1024]{0:T(1024)} %get-tuple-element.430, ...), kind=kOutput, calls=%fused_computation.14.clone.1 | convolution fusion | flops 410255360 | bytes 1061888 | tf_op jit(solution)/shard_map/while/body/eval_jaxpr/dot_general | solution.py:106
  73.8 3.8 %fusion.70 = f32[8,512,128]{2,1,0:T(8,128)} fusion(f32[8,512,128]{2,1,0:T(8,128)} %get-tuple-element.417, s32[]{:T(128)S(6)} %copy.14, bf16[1024,256]{1,0:T(8,128)(2,1)} %get-tuple-element.428, f32[1024]{0:T(1024)} %get-tuple-element.429, f32[1024]{0:T(1024)} %get-tuple-element.426, s32[1024]{0:T(1024)} %get-tuple-element.430, ...), kind=kOutput, calls=%fused_computation.14.clone.1 | convolution fusion | flops 410255360 | bytes 1061888 | tf_op jit(solution)/shard_map/while/body/eval_jaxpr/dot_general | solution.py:106
  77.6 3.8 %fusion.70 = f32[8,512,128]{2,1,0:T(8,128)} fusion(f32[8,512,128]{2,1,0:T(8,128)} %get-tuple-element.417, s32[]{:T(128)S(6)} %copy.14, bf16[1024,256]{1,0:T(8,128)(2,1)} %get-tuple-element.428, f32[1024]{0:T(1024)} %get-tuple-element.429, f32[1024]{0:T(1024)} %get-tuple-element.426, s32[1024]{0:T(1024)} %get-tuple-element.430, ...), kind=kOutput, calls=%fused_computation.14.clone.1 | convolution fusion | flops 410255360 | bytes 1061888 | tf_op jit(solution)/shard_map/while/body/eval_jaxpr/dot_general | solution.py:106
  81.4 3.8 %fusion.70 = f32[8,512,128]{2,1,0:T(8,128)} fusion(f32[8,512,128]{2,1,0:T(8,128)} %get-tuple-element.417, s32[]{:T(128)S(6)} %copy.14, bf16[1024,256]{1,0:T(8,128)(2,1)} %get-tuple-element.428, f32[1024]{0:T(1024)} %get-tuple-element.429, f32[1024]{0:T(1024)} %get-tuple-element.426, s32[1024]{0:T(1024)} %get-tuple-element.430, ...), kind=kOutput, calls=%fused_computation.14.clone.1 | convolution fusion | flops 410255360 | bytes 1061888 | tf_op jit(solution)/shard_map/while/body/eval_jaxpr/dot_general | solution.py:106
  85.9 96.4 %all-reduce.2.cloned.1.call-done = f32[4096,128]{1,0:T(8,128)} async-done(((f32[4096,128]{1,0:T(8,128)}), f32[4096,128]{1,0:T(8,128)}) %all-reduce.2.cloned.1.call-update) | async-done | bytes 2097168 | tf_op jit(solution)/shard_map/psum | solution.py:145
  182.2 3.0 %fusion.50 = (f32[]{:T(128)}, f32[4096]{0:T(1024)S(1)}) fusion(f32[4096,128]{1,0:T(8,128)} %all-reduce.2.cloned.1.call-done), kind=kLoop, calls=%fused_computation.73 | loop fusion | flops 1044479 | bytes 2113540 | tf_op jit(solution)/shard_map/reduce_sum | solution.py:51
  197.6 47.0 %while.29 = (s32[]{:T(128)}, f32[1024,256]{1,0:T(8,128)S(1)}, f32[1024]{0:T(1024)S(1)}, f32[1024]{0:T(1024)S(1)}, bf16[8,512,128]{2,1,0:T(8,128)(2,1)S(1)}, /*in...) while((s32[]{:T(128)}, f32[1024,256]{1,0:T(8,128)S(1)}, ...), condition=%wide.region_16.17_spmd.clone, body=%wide.region_14.16_spmd.clone.sunk | while | flops 681313280 | bytes 15892648 | solution.py:130
  198.7 2.8 fusion.76
  204.5 2.8 fusion.76
  210.4 2.8 fusion.76
  213.2 2.0 convolution_add_fusion.2
  216.3 2.8 fusion.76
  222.2 2.8 fusion.76
  225.0 2.0 convolution_add_fusion.2
  228.1 2.8 fusion.76
  233.9 2.8 fusion.76
  239.8 2.8 fusion.76
  247.4 30.9 %psum.15 = f32[]{:T(128)} all-reduce(f32[]{:T(128)S(6)} %add.106), channel_id=1, replica_groups=mesh['groups'=2,'asset'=16] {'asset'}, use_global_device_ids=true, to_apply=%region_19.20 | all-reduce | flops 1 | bytes 8 | tf_op jit(solution)/shard_map/psum | solution.py:154
  (75 shorter events, 36.3 us)
Async XLA Ops:
  7.2 0.9 copy-start
  7.2 47.8 %all-gather.2.cloned.1.call-start = ((), (), s32[]{:S(2)}) async-start(), calls=%async_computation | async-start | bytes 2228224 | tf_op jit(solution)/shard_map/all_gather | solution.py:143
  9.8 172.4 %all-reduce.2.cloned.1.call-start = ((), (), s32[]{:S(2)}) async-start(), calls=%async_computation.1 | async-start | bytes 4194304 | tf_op jit(solution)/shard_map/psum | solution.py:145
  85.2 100.7 %copy-start.5 = (s32[4096]{0:T(1024)S(1)}, s32[4096]{0:T(1024)}, u32[]{:S(2)}) copy-start(s32[4096]{0:T(1024)} %param.18) | copy-start | bytes 49156
  85.2 103.4 %copy-start.6 = (f32[128]{0:T(128)S(1)}, f32[128]{0:T(128)}, u32[]{:S(2)}) copy-start(f32[128]{0:T(128)} %param.19) | copy-start | bytes 1540
  182.2 6.3 %copy-start.1 = (f32[4096,128]{1,0:T(8,128)S(1)}, f32[4096,128]{1,0:T(8,128)}, u32[]{:S(2)}) copy-start(f32[4096,128]{1,0:T(8,128)} %all-reduce.2.cloned.1.call-done) | copy-start | bytes 6291460
  185.2 12.4 %copy-start.2 = (s32[1024]{0:T(1024)S(1)}, s32[1024]{0:T(1024)}, u32[]{:S(2)}) copy-start(s32[1024]{0:T(1024)} %get-tuple-element.474) | copy-start | bytes 12292
  185.2 12.4 %copy-start.3 = (f32[1024]{0:T(1024)S(1)}, f32[1024]{0:T(1024)}, u32[]{:S(2)}) copy-start(f32[1024]{0:T(1024)} %get-tuple-element.475) | copy-start | bytes 12292
  185.2 12.4 %copy-start.4 = (f32[1024]{0:T(1024)S(1)}, f32[1024]{0:T(1024)}, u32[]{:S(2)}) copy-start(f32[1024]{0:T(1024)} %get-tuple-element.476) | copy-start | bytes 12292
  197.6 1.0 copy-start.7
  203.5 1.0 copy-start.7
  209.4 1.0 copy-start.7
  215.3 1.0 copy-start.7
  221.1 1.0 copy-start.7
  227.0 1.0 copy-start.7
  232.9 1.0 copy-start.7
  238.8 1.0 copy-start.7
Sparse Core Ops, SparseCore 0:
  10.7 44.1 all-gather.1
  85.4 96.8 all-reduce.1
where the time goes:
time: 290 us; the launch traced here: 289 us
  waiting for transfers between devices  141 us (49%)
  matrix products  74.8 us (26%)
  blocking collectives  30.9 us (11%)
  between operations  20.2 us (7%)
  other arithmetic  16.1 us (6%)
  local copies, waits for them, and re-layouts  4.69 us (2%)
    psum x1, waiting for transfers between devices, shards(): desk_pnl = lax.psum(partial_value, 'asset')  96.4 us
    all_gather x1, waiting for transfers between devices, shards(): shocks = lax.all_gather(local_shocks, 'asset', axis=0, tiled=True)  45 us
    psum x1, blocking collectives, shards(): lax.psum(jnp.sum(grad_load * grad_load) + jnp.sum(grad_conv * grad_conv),...  30.9 us
    dot_general x8, matrix products, pnl_one_block(): return jnp.dot(held, table, preferred_element_type=jnp.float32)  30.3 us
    dot_general x8, matrix products, exposure_of(): lax.dot_general(shock_rows, loadings, (((1,), (1,)), ((), ())), preferred...  22.1 us
    dot_general x8, matrix products, grad_one_block(): lax.dot_general(grad_exposure, shock_block, (((0,), (0,)), ((), ())), pre...  16.2 us
  transfers between devices with their start and end apart: 2, of which 2 were waited for; matrix products, arithmetic and copies ran while one was open for 0% of the time, Pallas kernels for 0%

commit v1 on v0

v1 whole, which is shorter than its diff:
```python
import functools
import math

import jax
import jax.numpy as jnp
from jax import lax
from jax.experimental import pallas as pl
from jax.experimental.pallas import tpu as pltpu
from jax.sharding import PartitionSpec as P

DESKS = 128
BAND = 32
CENTER = 166
MESH = pl.DeviceIdType.MESH
F32 = jnp.float32
BF16 = jnp.bfloat16
NT = (((1,), (1,)), ((), ()))


def dot(left, right):
    return jnp.dot(left, right, preferred_element_type=F32)


def dot_nt(left, right):
    return lax.dot_general(left, right, NT, preferred_element_type=F32)


def halves(value):
    high = value.astype(BF16).astype(F32)
    return high, value - high


def stack_rows(rows, count):
    width = rows[0].shape[1]
    if count > len(rows):
        rows = list(rows) + [jnp.zeros((count - len(rows), width), F32)]
    return jnp.concatenate(rows, axis=0)


def total(value):
    return jnp.sum(jnp.sum(value, axis=1, keepdims=True), axis=0, keepdims=True)


def position_of(chip, chips, folded):
    if not folded:
        return chip
    return chip // 2 + (chip % 2) * (chips - 1 - 2 * (chip // 2))


def chip_at(position, chips, folded):
    position = (position + chips) % chips
    if not folded:
        return position
    back = position // (chips // 2)
    return 2 * position + back * (2 * chips - 1 - 4 * position)


def kernel(
    n,
    folded,
    draws_ref,
    mix_ref,
    load_ref,
    conv_ref,
    hold_ref,
    desk_ref,
    ranks_ref,
    prices_ref,
    alloc_ref,
    grad_ref,
    gconv_ref,
    landed,
    shocks,
    tanhs,
    bends,
    scaled,
    table,
    columns,
    first_rows,
    part,
    gathered,
    sums,
    loss_all,
    valued_all,
    stat_rows,
    finals,
    ring_send,
    ring_recv,
    pair_send,
    pair_recv,
    part_send,
    part_recv,
    sums_send,
    sums_recv,
    fin_send,
    fin_recv,
    own_sem,
):
    me = lax.axis_index("asset")
    chips = n // 2
    core = me % 2
    chip = me // 2
    where = position_of(chip, chips, folded)
    partner = chip * 2 + (1 - core)
    right = chip_at(where + 1, chips, folded) * 2 + core
    left = chip_at(where - 1, chips, folded) * 2 + core
    rows, factors = draws_ref.shape
    block = 2 * rows
    scenarios = rows * n
    assets = load_ref.shape[0]
    tile = math.gcd(assets, 256)
    last = chips // 2
    half = rows // 2

    barrier = pltpu.get_barrier_semaphore()
    for other in (right, left, partner):
        pl.semaphore_signal(barrier, inc=1, device_id={"asset": other}, device_id_type=MESH)
    pl.semaphore_wait(barrier, 3)

    def shard_at(step):
        return chip_at(where + step, chips, folded) * 2 + core

    def ring_copy(direction, step):
        shard = shard_at(-direction * (step - 1))
        lane = 0 if direction == 1 else 1
        source = draws_ref if step == 1 else landed.at[shard]
        target = landed.at[shard]
        if step == last:
            piece = pl.ds(0 if direction == 1 else half, half)
            source, target = source.at[piece], target.at[piece]
        return pltpu.make_async_remote_copy(
            src_ref=source,
            dst_ref=target,
            send_sem=ring_send.at[lane, step - 1],
            recv_sem=ring_recv.at[lane, step - 1],
            device_id={"asset": right if direction == 1 else left},
            device_id_type=MESH,
        )

    def pair_copy(step):
        shard = shard_at(step)
        source = draws_ref if step == 0 else landed.at[shard]
        return pltpu.make_async_remote_copy(
            src_ref=source,
            dst_ref=landed.at[shard],
            send_sem=pair_send.at[step + last],
            recv_sem=pair_recv.at[step + last],
            device_id={"asset": partner},
            device_id_type=MESH,
        )

    started = []

    def start(copy):
        copy.start()
        started.append(copy)
        return copy

    ring = {}
    for direction in (1, -1):
        ring[direction, 1] = start(ring_copy(direction, 1))
    pair = {0: start(pair_copy(0))}
    own = pltpu.make_async_copy(draws_ref, landed.at[me], own_sem)
    own.start()

    conv = conv_ref[...]
    hold = hold_ref[...]
    desk = desk_ref[...]
    same = lax.broadcasted_iota(jnp.int32, (DESKS, assets), 0) == desk
    table[...] = same.astype(F32).astype(BF16)
    price_high, price_rest = halves(prices_ref[...])
    price_mid, price_low = halves(price_rest)
    price_rows = stack_rows([price_high, price_mid, price_low], 16).astype(BF16)
    price = jnp.sum(dot(price_rows, table[...]), axis=0, keepdims=True)
    columns[...] = jnp.transpose(stack_rows([conv, hold, price], 128))
    linear = dot(
        stack_rows([*halves(hold), *halves(hold * price)], 16).astype(BF16), load_ref[...]
    )
    linear_loss = linear[0:1] + linear[1:2]
    linear_value = linear[2:3] + linear[3:4]
    linear_rows = stack_rows([*halves(linear_loss), *halves(linear_value)], 16).astype(BF16)
    bent = hold * conv
    first_rows[...] = stack_rows([*halves(bent), *halves(bent * price)], 16).astype(BF16)

    def forward(step):
        place = chip_at(where + step, chips, folded)
        draws = landed[pl.ds(place * 2, 2)].reshape(block, factors)
        shock = dot(draws, mix_ref[...]).astype(BF16)
        at = pl.multiple_of(place * block, block)
        shocks[pl.ds(at, block), :] = shock
        result = dot_nt(linear_rows, shock)
        for first in range(0, assets, tile):
            exposure = dot_nt(load_ref[pl.ds(first, tile), :], shock)
            tanhs[pl.ds(first, tile), pl.ds(at, block)] = jnp.tanh(exposure).astype(BF16)
            size = jnp.abs(exposure)
            bend = (size + jnp.log(1.0 + jnp.exp(-2.0 * size)) - math.log(2.0)).astype(BF16)
            bends[pl.ds(first, tile), pl.ds(at, block)] = bend
            result = result + dot(first_rows[:, first : first + tile], bend)
        loss = -(result[0:1] + result[1:2])
        value = result[2:3] + result[3:4]
        both = jnp.concatenate([loss, value], axis=0)
        part[place * 2] = both[:, 0:rows]
        part[place * 2 + 1] = both[:, rows:block]

    own.wait()
    pair[0].wait_recv()
    pending = [0]
    for step in range(1, last + 1):
        arrived = (-step, step) if step < last else (step,)
        for direction in (1, -1):
            ring[direction, step].wait_recv()
            if step < last:
                ring[direction, step + 1] = start(ring_copy(direction, step + 1))
                pair[-direction * step] = start(pair_copy(-direction * step))
        if step == last:
            pair[last] = start(pair_copy(last))
        for ready in pending:
            forward(ready)
        for ready in arrived:
            pair[ready].wait_recv()
        pending = arrived
    for ready in pending:
        forward(ready)
    for copy in started:
        copy.wait_send()

    def to_all(source, target, send_sem, recv_sem):
        copies = []
        for offset in range(1, n):
            other = (me + offset) % n
            copies.append(
                pltpu.make_async_remote_copy(
                    src_ref=source(other),
                    dst_ref=target(offset),
                    send_sem=send_sem.at[offset],
                    recv_sem=recv_sem.at[offset],
                    device_id={"asset": other},
                    device_id_type=MESH,
                )
            )
        for copy in copies:
            copy.start()
        return copies

    copies = to_all(lambda other: part.at[other], lambda offset: gathered.at[offset], part_send, part_recv)
    mine = part[me]
    for copy in copies:
        copy.wait()
    for offset in range(1, n):
        mine = mine + gathered[offset]
    sums[me] = mine
    copies = to_all(lambda other: sums.at[me], lambda offset: sums.at[me], sums_send, sums_recv)
    for copy in copies:
        copy.wait()
    for device in range(n):
        entry = sums[device]
        loss_all[pl.ds(device, 1), :] = entry[0:1]
        valued_all[pl.ds(device, 1), :] = entry[1:2]

    losses = loss_all[...]
    valued = valued_all[...]
    offsets = (ranks_ref[...].astype(F32) - CENTER) / BAND
    counter = (
        lax.broadcasted_iota(jnp.int32, (n, rows), 0) * rows
        + lax.broadcasted_iota(jnp.int32, (n, rows), 1)
    )
    every = (counter.astype(F32) - CENTER) / BAND
    bell = jnp.exp(-0.5 * offsets * offsets) / total(jnp.exp(-0.5 * every * every))
    quantile = total(bell * losses)
    centred = losses - total(losses) / scenarios
    smoothing = 0.3 * jnp.sqrt(total(centred * centred) / scenarios + 1e-06)
    scores = (losses - quantile) / smoothing
    weights = jax.nn.sigmoid(scores)
    weight_total = total(weights)
    objective = -total(weights * valued) / weight_total
    slopes = (-valued - objective) / weight_total * weights * (1.0 - weights)
    grad_quant = -total(slopes) / smoothing
    grad_band = -total(slopes * scores) / smoothing
    grad_loss = (
        slopes / smoothing
        + bell * grad_quant
        + grad_band * 0.09 * centred / (scenarios * smoothing)
    )
    share = weights * (scenarios / weight_total)
    grad_loss = scenarios * grad_loss

    wide = -(-rows // 128) * 128
    upright = stack_rows([share, grad_loss], -(-2 * n // 128) * 128)
    if wide > rows:
        upright = jnp.concatenate(
            [upright, jnp.zeros((upright.shape[0], wide - rows), F32)], axis=1
        )
    upright = jnp.transpose(upright)
    for device in range(n):
        piece = shocks[device * rows : (device + 1) * rows, :].astype(F32)
        for side in range(2):
            scale = upright[0:rows, side * n + device : side * n + device + 1]
            scaled[
                device * rows : (device + 1) * rows, side * factors : (side + 1) * factors
            ] = (piece * scale).astype(BF16)
    pieces = [*halves(share), *halves(grad_loss)]
    for place in range(chips):
        lines = [
            jnp.concatenate(
                [piece[2 * place : 2 * place + 1], piece[2 * place + 1 : 2 * place + 2]], axis=1
            )
            for piece in pieces
        ]
        stat_rows[:, place * block : (place + 1) * block] = stack_rows(lines, 16).astype(BF16)

    plain = dot(stat_rows[...], shocks[...])
    plain_share = plain[0:1] + plain[1:2]
    plain_loss = plain[2:3] + plain[3:4]
    plain_rows = stack_rows([*halves(plain_share)], 16).astype(BF16)

    squares = jnp.zeros((1, 1), F32)
    allocation = jnp.zeros((1, DESKS), F32)
    for first in range(0, assets, tile):
        span = slice(first, first + tile)
        both = dot(tanhs[span, :], scaled[...])
        conv_column = columns[span, 0:1]
        hold_column = columns[span, 1:2]
        price_column = columns[span, 2:3]
        raw = -hold_column * (
            price_column * (plain_share + conv_column * both[:, 0:factors])
            + (plain_loss + conv_column * both[:, factors:])
        )
        grad_ref[span, :] = raw
        squares = squares + total(raw * raw)
        sides = dot_nt(stat_rows[...], bends[span, :])
        side_share = sides[0:1] + sides[1:2]
        side_loss = sides[2:3] + sides[3:4]
        hold_row = hold_ref[:, span]
        raw_conv = -hold_row * (price[:, span] * side_share + side_loss)
        gconv_ref[:, span] = raw_conv
        squares = squares + total(raw_conv * raw_conv)
        linear_share = dot_nt(plain_rows, load_ref[span, :])
        using = hold_row * (
            linear_share[0:1] + linear_share[1:2] + conv_ref[:, span] * side_share
        )
        using_rows = stack_rows([*halves(using)], 16).astype(BF16)
        found = dot_nt(using_rows, table[:, span])
        allocation = allocation - (found[0:1] + found[1:2])
    finals[me] = stack_rows(
        [allocation * (1.0 / scenarios), jnp.broadcast_to(squares, (1, DESKS))], 8
    )
    copies = to_all(lambda other: finals.at[me], lambda offset: finals.at[me], fin_send, fin_recv)
    for copy in copies:
        copy.wait()
    final = finals[0]
    for device in range(1, n):
        final = final + finals[device]
    alloc_ref[...] = final[0:1]
    entries = assets * n * (factors + 1)
    factor = lax.rsqrt(final[1:2, 0:1] / entries + 1e-06)
    gconv_ref[...] = gconv_ref[...] * factor
    grad_ref[...] = grad_ref[...] * factor


def shards(
    folded, n, scen_draws, factor_mix, loadings, convexity, holdings, desk_map, ranks, desk_prices
):
    rows, factors = scen_draws.shape
    assets = loadings.shape[0]
    scenarios = rows * n
    last = n // 4
    dma = pltpu.SemaphoreType.DMA
    vmem = pl.BlockSpec(memory_space=pltpu.VMEM)
    allocation, grad_load, grad_conv = pl.pallas_call(
        functools.partial(kernel, n, folded),
        out_shape=(
            jax.ShapeDtypeStruct((1, DESKS), F32),
            jax.ShapeDtypeStruct((assets, factors), F32),
            jax.ShapeDtypeStruct((1, assets), F32),
        ),
        in_specs=[vmem] * 8,
        out_specs=(vmem,) * 3,
        scratch_shapes=[
            pltpu.VMEM((n, rows, factors), BF16),
            pltpu.VMEM((scenarios, factors), BF16),
            pltpu.VMEM((assets, scenarios), BF16),
            pltpu.VMEM((assets, scenarios), BF16),
            pltpu.VMEM((scenarios, 2 * factors), BF16),
            pltpu.VMEM((DESKS, assets), BF16),
            pltpu.VMEM((assets, 128), F32),
            pltpu.VMEM((16, assets), BF16),
            pltpu.VMEM((n, 2, rows), F32),
            pltpu.VMEM((n, 2, rows), F32),
            pltpu.VMEM((n, 2, rows), F32),
            pltpu.VMEM((n, rows), F32),
            pltpu.VMEM((n, rows), F32),
            pltpu.VMEM((16, scenarios), BF16),
            pltpu.VMEM((n, 8, DESKS), F32),
            dma((2, last)),
            dma((2, last)),
            dma((2 * last + 1,)),
            dma((2 * last + 1,)),
            dma((n,)),
            dma((n,)),
            dma((n,)),
            dma((n,)),
            dma((n,)),
            dma((n,)),
            dma,
        ],
        compiler_params=pltpu.CompilerParams(
            collective_id=0, has_side_effects=True, vmem_limit_bytes=60 * 1024 * 1024
        ),
        name="tail_step",
    )(
        scen_draws,
        factor_mix,
        loadings,
        convexity.reshape(1, assets),
        holdings.reshape(1, assets),
        desk_map.reshape(1, assets),
        ranks.reshape(n, rows),
        desk_prices.reshape(1, DESKS),
    )
    return (allocation.reshape(DESKS), grad_load, grad_conv.reshape(assets))


def chip_distance(one, two):
    return sum(abs(a - b) for a, b in zip(one, two))


def ring_is_folded(mesh):
    try:
        places = [tuple(device.coords) for device in mesh.devices.reshape(-1, mesh.shape["asset"])[0]]
    except AttributeError:
        return False
    places = places[::2]
    chips = len(places)
    if chips % 2:
        return False
    costs = []
    for folded in (False, True):
        order = [places[chip_at(position, chips, folded)] for position in range(chips)]
        hops = [chip_distance(order[i], order[i + 1]) for i in range(chips - 1)]
        costs.append(sum(hops))
    return costs[1] < costs[0]


def solution(mesh):
    placed = (
        P(("groups", "asset"), None),
        P(),
        P(("groups", "asset"), None),
        P(("groups", "asset")),
        P(("groups", "asset")),
        P(("groups", "asset")),
        P("groups"),
        P("groups"),
    )
    return jax.shard_map(
        functools.partial(shards, ring_is_folded(mesh), mesh.shape["asset"]),
        mesh=mesh,
        in_specs=placed,
        out_specs=(P("groups"), P(("groups", "asset"), None), P(("groups", "asset"))),
        check_vma=False,
    )
```

time: 290 us -> 57.2 us (0.20)
  waiting for transfers between devices: 141 us -> 0 us
  matrix products: 74.8 us -> 0 us
  Pallas kernels: 0 us -> 51.1 us
  blocking collectives: 30.9 us -> 0 us
  between operations: 20.2 us -> 0.65 us
  other arithmetic: 16.1 us -> 0 us
    psum x1 -> x0, waiting for transfers between devices: 96.4 us -> none  [shards(): desk_pnl = lax.psum(partial_value, 'asset')]
    dot_general x33 -> x0, matrix products: 74.8 us -> none  [the longest x8 30.3 us: pnl_one_block(): return jnp.dot(held, table, preferred_element_type=jnp.float32)]
    pallas_call x0 -> x1, Pallas kernels: none -> 51.1 us  [shards(): pl.pallas_call(functools.partial(kernel, n, folded), out_shape=(jax.Shape...]
    all_gather x1 -> x0, waiting for transfers between devices: 45 us -> none  [shards(): shocks = lax.all_gather(local_shocks, 'asset', axis=0, tiled=True)]
    psum x1 -> x0, blocking collectives: 30.9 us -> none  [shards(): lax.psum(jnp.sum(grad_load * grad_load) + jnp.sum(grad_conv * grad_conv),...]
    reduce_sum x8 -> x0, other arithmetic: 10.1 us -> none  [the longest x1 2.95 us: tail_core(): average = jnp.mean(losses)]
    while x16 -> x0, local copies, waits for them, and re-layouts: 3.8 us -> none
    unnamed x14 -> x7, local copies, waits for them, and re-layouts: 0.88 us -> 3.94 us
  transfers between devices with their start and end apart: 2 -> 0, of which waited for: 2 -> 0; matrix products, arithmetic and copies ran while one was open for 0% -> 0% of each run, Pallas kernels for 0% -> 0%
where the time goes in v1:
time: 57.2 us; the launch traced here: 57 us
  Pallas kernels  51.1 us (89%)
  local copies, waits for them, and re-layouts  5.27 us (9%)
  between operations  0.65 us (1%)
    pallas_call x1, Pallas kernels, shards(): pl.pallas_call(functools.partial(kernel, n, folded), out_shape=(jax.Shape...  51.1 us
    unnamed x7, local copies, waits for them, and re-layouts  3.94 us
    reshape x1, local copies, waits for them, and re-layouts, shards(): ranks.reshape(n, rows)  1.33 us

profile of v1, /device:TPU:0, one launch (start us, length us, event | category | flops | bytes accessed | tf_op | source)
XLA Modules:
  0.0 57.0 jit_solution(6537160762168372886)
XLA Ops:
  0.6 1.3 %reshape.30.ranks_ref = s32[16,256]{1,0:T(8,128)} reshape(s32[4096]{0:T(1024)} %param.14) | data formatting | bytes 32768 | tf_op jit(solution)/shard_map/reshape | solution.py:417
  2.0 51.1 %tail_step.1 = (f32[1,128]{1,0:T(1,128)}, f32[1024,256]{1,0:T(8,128)}, f32[1,1024]{1,0:T(1,128)}) custom-call(bf16[256,256]{1,0:T(8,128)(2,1)} %draws_ref.1, bf16[256,256]{1,0:T(8,128)(2,1)} %mix_ref.1, bf16[1024,256]{1,0:T(8,128)(2,1)} %load_ref.1, f32[1,1024]{1,0:T(1,128)} %bitcast.6, f32[1,1024]{1,0:T(1,128)} %bitcast.7, s32[1,1024]{1,0:T(1,128)} %bitcast.8, ...), custom_call_target="tpu_custom_call" | custom-call | tf_op jit(solution)/shard_map/tail_step/pallas_call | solution.py:369
  53.0 0.0 copy-start.1
  53.1 0.6 copy-done.1
  53.6 0.5 copy.14
  54.1 0.0 copy-start
  54.1 2.3 %copy.15 = f32[1024,256]{1,0:T(8,128)} copy(f32[1024,256]{1,0:T(8,128)} %get-tuple-element.13) | data formatting | bytes 2097152
  56.4 0.0 copy-done
  56.4 0.6 %copy.16 = f32[1024]{0:T(1024)} copy(f32[1024]{0:T(1024)S(1)} %bitcast.9) | data formatting | bytes 8192
Async XLA Ops:
  53.0 0.6 %copy-start.1 = (f32[1,128]{1,0:T(1,128)S(1)}, f32[1,128]{1,0:T(1,128)}, u32[]{:S(2)}) copy-start(f32[1,128]{1,0:T(1,128)} %get-tuple-element.6) | copy-start | bytes 1540
  54.1 2.3 %copy-start = (f32[1,1024]{1,0:T(1,128)S(1)}, f32[1,1024]{1,0:T(1,128)}, u32[]{:S(2)}) copy-start(f32[1,1024]{1,0:T(1,128)} %get-tuple-element.8) | copy-start | bytes 12292

commit v2 on v1

--- a/solution.py
+++ b/solution.py
@@ -11,6 +11,7 @@
 DESKS = 128
 BAND = 32
 CENTER = 166
+PIECES = 4
 MESH = pl.DeviceIdType.MESH
 F32 = jnp.float32
 BF16 = jnp.bfloat16
@@ -59,6 +60,16 @@
     n,
     folded,
     draws_ref,
+    mix_hbm,
+    load_hbm,
+    conv_hbm,
+    hold_hbm,
+    desk_hbm,
+    ranks_hbm,
+    prices_hbm,
+    final_ref,
+    raw_hbm,
+    raw_conv_hbm,
     mix_ref,
     load_ref,
     conv_ref,
@@ -66,7 +77,6 @@
     desk_ref,
     ranks_ref,
     prices_ref,
-    alloc_ref,
     grad_ref,
     gconv_ref,
     landed,
@@ -82,6 +92,7 @@
     sums,
     loss_all,
     valued_all,
+    ranks_all,
     stat_rows,
     finals,
     ring_send,
@@ -95,6 +106,8 @@
     fin_send,
     fin_recv,
     own_sem,
+    in_sems,
+    out_sems,
 ):
     me = lax.axis_index("asset")
     chips = n // 2
@@ -110,41 +123,57 @@
     assets = load_ref.shape[0]
     tile = math.gcd(assets, 256)
     last = chips // 2
-    half = rows // 2
+    part_rows = rows // PIECES
 
     barrier = pltpu.get_barrier_semaphore()
     for other in (right, left, partner):
         pl.semaphore_signal(barrier, inc=1, device_id={"asset": other}, device_id_type=MESH)
+    own = pltpu.make_async_copy(draws_ref, landed.at[me], own_sem)
+    own.start()
+    inputs = [
+        pltpu.make_async_copy(source, target, in_sems.at[index])
+        for index, (source, target) in enumerate(
+            [
+                (conv_hbm, conv_ref),
+                (hold_hbm, hold_ref),
+                (desk_hbm, desk_ref),
+                (prices_hbm, prices_ref),
+                (load_hbm, load_ref),
+                (mix_hbm, mix_ref),
+                (ranks_hbm, ranks_ref),
+            ]
+        )
+    ]
+    for copy in inputs:
+        copy.start()
     pl.semaphore_wait(barrier, 3)
 
     def shard_at(step):
         return chip_at(where + step, chips, folded) * 2 + core
 
-    def ring_copy(direction, step):
+    def ring_copy(direction, step, piece):
         shard = shard_at(-direction * (step - 1))
         lane = 0 if direction == 1 else 1
-        source = draws_ref if step == 1 else landed.at[shard]
-        target = landed.at[shard]
-        if step == last:
-            piece = pl.ds(0 if direction == 1 else half, half)
-            source, target = source.at[piece], target.at[piece]
+        span = pl.ds(piece * part_rows, part_rows)
+        source = draws_ref.at[span] if step == 1 else landed.at[shard, span]
         return pltpu.make_async_remote_copy(
             src_ref=source,
-            dst_ref=target,
-            send_sem=ring_send.at[lane, step - 1],
-            recv_sem=ring_recv.at[lane, step - 1],
+            dst_ref=landed.at[shard, span],
+            send_sem=ring_send.at[lane, step - 1, piece],
+            recv_sem=ring_recv.at[lane, step - 1, piece],
             device_id={"asset": right if direction == 1 else left},
             device_id_type=MESH,
         )
 
-    def pair_copy(step):
+    def pair_copy(step, piece):
         shard = shard_at(step)
-        source = draws_ref if step == 0 else landed.at[shard]
+        span = pl.ds(piece * part_rows, part_rows)
+        source = draws_ref.at[span] if step == 0 else landed.at[shard, span]
         return pltpu.make_async_remote_copy(
             src_ref=source,
-            dst_ref=landed.at[shard],
-            send_sem=pair_send.at[step + last],
-            recv_sem=pair_recv.at[step + last],
+            dst_ref=landed.at[shard, span],
+            send_sem=pair_send.at[step + last, piece],
+            recv_sem=pair_recv.at[step + last, piece],
             device_id={"asset": partner},
             device_id_type=MESH,
         )
@@ -156,12 +185,21 @@
         started.append(copy)
         return copy
 
+    def crossing(direction, step):
+        if step < last:
+            return range(PIECES)
+        return range(PIECES // 2) if direction == 1 else range(PIECES // 2, PIECES)
+
     ring = {}
-    for direction in (1, -1):
-        ring[direction, 1] = start(ring_copy(direction, 1))
-    pair = {0: start(pair_copy(0))}
-    own = pltpu.make_async_copy(draws_ref, landed.at[me], own_sem)
-    own.start()
+    pair = {}
+    for piece in range(PIECES):
+        for direction in (1, -1):
+            if piece in crossing(direction, 1):
+                ring[direction, 1, piece] = start(ring_copy(direction, 1, piece))
+    for piece in range(PIECES):
+        pair[0, piece] = start(pair_copy(0, piece))
+    for copy in inputs:
+        copy.wait()
 
     conv = conv_ref[...]
     hold = hold_ref[...]
@@ -183,6 +221,8 @@
     first_rows[...] = stack_rows([*halves(bent), *halves(bent * price)], 16).astype(BF16)
 
     def forward(step):
+        for piece in range(PIECES):
+            pair[step, piece].wait_recv()
         place = chip_at(where + step, chips, folded)
         draws = landed[pl.ds(place * 2, 2)].reshape(block, factors)
         shock = dot(draws, mix_ref[...]).astype(BF16)
@@ -196,31 +236,40 @@
             bend = (size + jnp.log(1.0 + jnp.exp(-2.0 * size)) - math.log(2.0)).astype(BF16)
             bends[pl.ds(first, tile), pl.ds(at, block)] = bend
             result = result + dot(first_rows[:, first : first + tile], bend)
+            if first + tile < assets:
+                yield
         loss = -(result[0:1] + result[1:2])
         value = result[2:3] + result[3:4]
         both = jnp.concatenate([loss, value], axis=0)
         part[place * 2] = both[:, 0:rows]
         part[place * 2 + 1] = both[:, rows:block]
+        yield
 
     own.wait()
-    pair[0].wait_recv()
+    parts = assets // tile
     pending = [0]
     for step in range(1, last + 1):
-        arrived = (-step, step) if step < last else (step,)
-        for direction in (1, -1):
-            ring[direction, step].wait_recv()
-            if step < last:
-                ring[direction, step + 1] = start(ring_copy(direction, step + 1))
-                pair[-direction * step] = start(pair_copy(-direction * step))
-        if step == last:
-            pair[last] = start(pair_copy(last))
-        for ready in pending:
-            forward(ready)
-        for ready in arrived:
-            pair[ready].wait_recv()
-        pending = arrived
-    for ready in pending:
-        forward(ready)
+        work = [(running, index) for running in map(forward, pending) for index in range(parts)]
+        slots = len(crossing(1, step))
+        for slot in range(slots):
+            for direction in (1, -1):
+                piece = crossing(direction, step)[slot]
+                ring[direction, step, piece].wait_recv()
+                behind = -direction * step if step < last else last
+                if step < last and piece in crossing(direction, step + 1):
+                    ring[direction, step + 1, piece] = start(
+                        ring_copy(direction, step + 1, piece)
+                    )
+                pair[behind, piece] = start(pair_copy(behind, piece))
+            for running, index in work[: -(-len(work) // (slots - slot))]:
+                next(running)
+            work = work[-(-len(work) // (slots - slot)) :]
+        pending = [-step, step] if step < last else [step]
+    for running in map(forward, pending):
+        for index in range(parts):
+            next(running)
+    for device in range(n):
+        ranks_all[pl.ds(device, 1), :] = ranks_ref[:, device * rows : (device + 1) * rows]
     for copy in started:
         copy.wait_send()
 
@@ -259,7 +308,7 @@
 
     losses = loss_all[...]
     valued = valued_all[...]
-    offsets = (ranks_ref[...].astype(F32) - CENTER) / BAND
+    offsets = (ranks_all[...].astype(F32) - CENTER) / BAND
     counter = (
         lax.broadcasted_iota(jnp.int32, (n, rows), 0) * rows
         + lax.broadcasted_iota(jnp.int32, (n, rows), 1)
@@ -313,6 +362,7 @@
     plain_loss = plain[2:3] + plain[3:4]
     plain_rows = stack_rows([*halves(plain_share)], 16).astype(BF16)
 
+    results = []
     squares = jnp.zeros((1, 1), F32)
     allocation = jnp.zeros((1, DESKS), F32)
     for first in range(0, assets, tile):
@@ -326,6 +376,13 @@
             + (plain_loss + conv_column * both[:, factors:])
         )
         grad_ref[span, :] = raw
+        copy = pltpu.make_async_copy(
+            grad_ref.at[pl.ds(first, tile)],
+            raw_hbm.at[pl.ds(first, tile)],
+            out_sems.at[first // tile],
+        )
+        copy.start()
+        results.append(copy)
         squares = squares + total(raw * raw)
         sides = dot_nt(stat_rows[...], bends[span, :])
         side_share = sides[0:1] + sides[1:2]
@@ -345,16 +402,22 @@
         [allocation * (1.0 / scenarios), jnp.broadcast_to(squares, (1, DESKS))], 8
     )
     copies = to_all(lambda other: finals.at[me], lambda offset: finals.at[me], fin_send, fin_recv)
-    for copy in copies:
+    copy = pltpu.make_async_copy(gconv_ref, raw_conv_hbm, out_sems.at[assets // tile])
+    copy.start()
+    results.append(copy)
+    for copy in copies + results:
         copy.wait()
     final = finals[0]
     for device in range(1, n):
         final = final + finals[device]
-    alloc_ref[...] = final[0:1]
-    entries = assets * n * (factors + 1)
-    factor = lax.rsqrt(final[1:2, 0:1] / entries + 1e-06)
-    gconv_ref[...] = gconv_ref[...] * factor
-    grad_ref[...] = grad_ref[...] * factor
+    final_ref[...] = final
+
+
+def scale_kernel(entries, final_ref, raw_ref, raw_conv_ref, alloc_ref, grad_ref, gconv_ref):
+    factor = lax.rsqrt(final_ref[1:2, 0:1] / entries + 1e-06)
+    alloc_ref[...] = final_ref[0:1, :]
+    gconv_ref[...] = raw_conv_ref[...] * factor
+    grad_ref[...] = raw_ref[...] * factor
 
 
 def shards(
@@ -364,18 +427,29 @@
     assets = loadings.shape[0]
     scenarios = rows * n
     last = n // 4
+    tiles = assets // math.gcd(assets, 256)
     dma = pltpu.SemaphoreType.DMA
     vmem = pl.BlockSpec(memory_space=pltpu.VMEM)
-    allocation, grad_load, grad_conv = pl.pallas_call(
+    anywhere = pl.BlockSpec(memory_space=pl.ANY)
+    final, raw, raw_conv = pl.pallas_call(
         functools.partial(kernel, n, folded),
         out_shape=(
-            jax.ShapeDtypeStruct((1, DESKS), F32),
+            jax.ShapeDtypeStruct((8, DESKS), F32),
             jax.ShapeDtypeStruct((assets, factors), F32),
             jax.ShapeDtypeStruct((1, assets), F32),
         ),
-        in_specs=[vmem] * 8,
-        out_specs=(vmem,) * 3,
+        in_specs=[anywhere] * 8,
+        out_specs=(vmem, anywhere, anywhere),
         scratch_shapes=[
+            pltpu.VMEM((factors, factors), BF16),
+            pltpu.VMEM((assets, factors), BF16),
+            pltpu.VMEM((1, assets), F32),
+            pltpu.VMEM((1, assets), F32),
+            pltpu.VMEM((1, assets), jnp.int32),
+            pltpu.VMEM((1, scenarios), jnp.int32),
+            pltpu.VMEM((1, DESKS), F32),
+            pltpu.VMEM((assets, factors), F32),
+            pltpu.VMEM((1, assets), F32),
             pltpu.VMEM((n, rows, factors), BF16),
             pltpu.VMEM((scenarios, factors), BF16),
             pltpu.VMEM((assets, scenarios), BF16),
@@ -389,12 +463,13 @@
             pltpu.VMEM((n, 2, rows), F32),
             pltpu.VMEM((n, rows), F32),
             pltpu.VMEM((n, rows), F32),
+            pltpu.VMEM((n, rows), jnp.int32),
             pltpu.VMEM((16, scenarios), BF16),
             pltpu.VMEM((n, 8, DESKS), F32),
-            dma((2, last)),
-            dma((2, last)),
-            dma((2 * last + 1,)),
-            dma((2 * last + 1,)),
+            dma((2, last, PIECES)),
+            dma((2, last, PIECES)),
+            dma((2 * last + 1, PIECES)),
+            dma((2 * last + 1, PIECES)),
             dma((n,)),
             dma((n,)),
             dma((n,)),
@@ -402,6 +477,8 @@
             dma((n,)),
             dma((n,)),
             dma,
+            dma((7,)),
+            dma((tiles + 1,)),
         ],
         compiler_params=pltpu.CompilerParams(
             collective_id=0, has_side_effects=True, vmem_limit_bytes=60 * 1024 * 1024
@@ -414,9 +491,25 @@
         convexity.reshape(1, assets),
         holdings.reshape(1, assets),
         desk_map.reshape(1, assets),
-        ranks.reshape(n, rows),
+        ranks.reshape(1, scenarios),
         desk_prices.reshape(1, DESKS),
     )
+    entries = assets * n * (factors + 1)
+    grid = 4
+    small = pl.BlockSpec((1, assets), lambda i: (0, 0))
+    wide = pl.BlockSpec((assets // grid, factors), lambda i: (i, 0))
+    allocation, grad_load, grad_conv = pl.pallas_call(
+        functools.partial(scale_kernel, entries),
+        grid=(grid,),
+        out_shape=(
+            jax.ShapeDtypeStruct((1, DESKS), F32),
+            jax.ShapeDtypeStruct((assets, factors), F32),
+            jax.ShapeDtypeStruct((1, assets), F32),
+        ),
+        in_specs=[pl.BlockSpec((8, DESKS), lambda i: (0, 0)), wide, small],
+        out_specs=(pl.BlockSpec((1, DESKS), lambda i: (0, 0)), wide, small),
+        name="scale_step",
+    )(final, raw, raw_conv)
     return (allocation.reshape(DESKS), grad_load, grad_conv.reshape(assets))
 
 

time: 57.2 us -> 53.7 us (0.939)
  local copies, waits for them, and re-layouts: 5.27 us -> 0 us
  Pallas kernels: 51.1 us -> 52.9 us
    unnamed x7 -> x0, local copies, waits for them, and re-layouts: 3.94 us -> none
    pallas_call x0 -> x1, Pallas kernels: none -> 3.46 us  [shards(): pl.pallas_call(functools.partial(scale_kernel, entries), grid=(grid,), ou...]
    pallas_call x1, Pallas kernels: 51.1 us -> 49.4 us  [shards(): pl.pallas_call(functools.partial(kernel, n, folded), out_shape=(jax.Shape...]
    reshape x1 -> x0, local copies, waits for them, and re-layouts: 1.33 us -> none  [shards(): ranks.reshape(n, rows)]
where the time goes in v2:
time: 53.7 us; the launch traced here: 53.5 us
  Pallas kernels  52.9 us (99%)
  between operations  0.64 us (1%)
    pallas_call x1, Pallas kernels, shards(): pl.pallas_call(functools.partial(kernel, n, folded), out_shape=(jax.Shape...  49.4 us
    pallas_call x1, Pallas kernels, shards(): pl.pallas_call(functools.partial(scale_kernel, entries), grid=(grid,), ou...  3.46 us

profile of v2, /device:TPU:0, one launch (start us, length us, event | category | flops | bytes accessed | tf_op | source)
XLA Modules:
  0.0 53.5 jit_solution(16998994253688718907)
XLA Ops:
  0.6 49.4 %tail_step.1 = (f32[8,128]{1,0:T(8,128)}, f32[1024,256]{1,0:T(8,128)}, f32[1,1024]{1,0:T(1,128)}) custom-call(bf16[256,256]{1,0:T(8,128)(2,1)} %draws_ref.1, bf16[256,256]{1,0:T(8,128)(2,1)} %mix_hbm.1, bf16[1024,256]{1,0:T(8,128)(2,1)} %load_hbm.1, f32[1,1024]{1,0:T(1,128)} %bitcast.8, f32[1,1024]{1,0:T(1,128)} %bitcast.9, s32[1,1024]{1,0:T(1,128)} %bitcast.10, ...), custom_call_target="tpu_custom_call" | custom-call | tf_op jit(solution)/shard_map/tail_step/pallas_call | solution.py:434
  50.1 3.5 %scale_step.1 = (f32[1,128]{1,0:T(1,128)}, f32[1024,256]{1,0:T(8,128)}, f32[1,1024]{1,0:T(1,128)}) custom-call(f32[8,128]{1,0:T(8,128)} %get-tuple-element.9.final_ref, f32[1024,256]{1,0:T(8,128)} %get-tuple-element.10.raw_ref, f32[1,1024]{1,0:T(1,128)} %get-tuple-element.11.raw_conv_ref), custom_call_target="tpu_custom_call" | custom-call | tf_op jit(solution)/shard_map/scale_step/pallas_call | solution.py:501

commit v3 on v2

--- a/solution.py
+++ b/solution.py
@@ -413,11 +413,29 @@
     final_ref[...] = final
 
 
-def scale_kernel(entries, final_ref, raw_ref, raw_conv_ref, alloc_ref, grad_ref, gconv_ref):
+def scale_kernel(
+    entries, final_ref, raw_conv_ref, raw_hbm, alloc_ref, gconv_ref, grad_hbm, held, in_sems, out_sems
+):
+    tile = held.shape[1]
+    count = held.shape[0]
+    reads = [
+        pltpu.make_async_copy(raw_hbm.at[pl.ds(i * tile, tile)], held.at[i], in_sems.at[i])
+        for i in range(count)
+    ]
+    for copy in reads:
+        copy.start()
     factor = lax.rsqrt(final_ref[1:2, 0:1] / entries + 1e-06)
     alloc_ref[...] = final_ref[0:1, :]
     gconv_ref[...] = raw_conv_ref[...] * factor
-    grad_ref[...] = raw_ref[...] * factor
+    writes = []
+    for i in range(count):
+        reads[i].wait()
+        held[i] = held[i] * factor
+        copy = pltpu.make_async_copy(held.at[i], grad_hbm.at[pl.ds(i * tile, tile)], out_sems.at[i])
+        copy.start()
+        writes.append(copy)
+    for copy in writes:
+        copy.wait()
 
 
 def shards(
@@ -495,21 +513,22 @@
         desk_prices.reshape(1, DESKS),
     )
     entries = assets * n * (factors + 1)
-    grid = 4
-    small = pl.BlockSpec((1, assets), lambda i: (0, 0))
-    wide = pl.BlockSpec((assets // grid, factors), lambda i: (i, 0))
-    allocation, grad_load, grad_conv = pl.pallas_call(
+    allocation, grad_conv, grad_load = pl.pallas_call(
         functools.partial(scale_kernel, entries),
-        grid=(grid,),
         out_shape=(
             jax.ShapeDtypeStruct((1, DESKS), F32),
+            jax.ShapeDtypeStruct((1, assets), F32),
             jax.ShapeDtypeStruct((assets, factors), F32),
-            jax.ShapeDtypeStruct((1, assets), F32),
         ),
-        in_specs=[pl.BlockSpec((8, DESKS), lambda i: (0, 0)), wide, small],
-        out_specs=(pl.BlockSpec((1, DESKS), lambda i: (0, 0)), wide, small),
+        in_specs=[vmem, vmem, anywhere],
+        out_specs=(vmem, vmem, anywhere),
+        scratch_shapes=[
+            pltpu.VMEM((tiles, assets // tiles, factors), F32),
+            dma((tiles,)),
+            dma((tiles,)),
+        ],
         name="scale_step",
-    )(final, raw, raw_conv)
+    )(final, raw_conv, raw)
     return (allocation.reshape(DESKS), grad_load, grad_conv.reshape(assets))
 
 

time: 53.7 us -> 53.7 us (level)
  no operation moved by 1% of the time
where the time goes in v3:
time: 53.7 us; the launch traced here: 53.5 us
  Pallas kernels  52.7 us (98%)
  between operations  0.8 us (1%)
    pallas_call x1, Pallas kernels, shards(): pl.pallas_call(functools.partial(kernel, n, folded), out_shape=(jax.Shape...  49.4 us
    pallas_call x1, Pallas kernels, shards(): pl.pallas_call(functools.partial(scale_kernel, entries), out_shape=(jax.S...  3.28 us

profile of v3, /device:TPU:0, one launch (start us, length us, event | category | flops | bytes accessed | tf_op | source)
XLA Modules:
  0.0 53.5 jit_solution(642399539755539601)
XLA Ops:
  0.6 49.4 %tail_step.1 = (f32[8,128]{1,0:T(8,128)}, f32[1024,256]{1,0:T(8,128)}, f32[1,1024]{1,0:T(1,128)}) custom-call(bf16[256,256]{1,0:T(8,128)(2,1)} %draws_ref.1, bf16[256,256]{1,0:T(8,128)(2,1)} %mix_hbm.1, bf16[1024,256]{1,0:T(8,128)(2,1)} %load_hbm.1, f32[1,1024]{1,0:T(1,128)} %bitcast.8, f32[1,1024]{1,0:T(1,128)} %bitcast.9, s32[1,1024]{1,0:T(1,128)} %bitcast.10, ...), custom_call_target="tpu_custom_call" | custom-call | tf_op jit(solution)/shard_map/tail_step/pallas_call | solution.py:452
  50.1 3.3 %scale_step.1 = (f32[1,128]{1,0:T(1,128)}, f32[1,1024]{1,0:T(1,128)}, f32[1024,256]{1,0:T(8,128)}) custom-call(f32[8,128]{1,0:T(8,128)} %get-tuple-element.9.final_ref, f32[1,1024]{1,0:T(1,128)} %get-tuple-element.10.raw_conv_ref, f32[1024,256]{1,0:T(8,128)} %get-tuple-element.11.raw_hbm), custom_call_target="tpu_custom_call" | custom-call | tf_op jit(solution)/shard_map/scale_step/pallas_call | solution.py:516

commit v4 on v2

--- a/solution.py
+++ b/solution.py
@@ -220,6 +220,18 @@
     bent = hold * conv
     first_rows[...] = stack_rows([*halves(bent), *halves(bent * price)], 16).astype(BF16)
 
+    parted = []
+
+    def part_copy(other, offset):
+        return pltpu.make_async_remote_copy(
+            src_ref=part.at[other],
+            dst_ref=gathered.at[offset],
+            send_sem=part_send.at[offset],
+            recv_sem=part_recv.at[offset],
+            device_id={"asset": other},
+            device_id_type=MESH,
+        )
+
     def forward(step):
         for piece in range(PIECES):
             pair[step, piece].wait_recv()
@@ -243,6 +255,10 @@
         both = jnp.concatenate([loss, value], axis=0)
         part[place * 2] = both[:, 0:rows]
         part[place * 2 + 1] = both[:, rows:block]
+        for other in [partner] if step == 0 else [place * 2, place * 2 + 1]:
+            copy = part_copy(other, (other - me + n) % n)
+            copy.start()
+            parted.append(copy)
         yield
 
     own.wait()
@@ -291,10 +307,11 @@
             copy.start()
         return copies
 
-    copies = to_all(lambda other: part.at[other], lambda offset: gathered.at[offset], part_send, part_recv)
     mine = part[me]
-    for copy in copies:
-        copy.wait()
+    for offset in range(1, n):
+        part_copy((me + offset) % n, offset).wait_recv()
+    for copy in parted:
+        copy.wait_send()
     for offset in range(1, n):
         mine = mine + gathered[offset]
     sums[me] = mine

time: 53.7 us -> 53.6 us (level)
  no operation moved by 1% of the time
where the time goes in v4:
time: 53.6 us; the launch traced here: 53.5 us
  Pallas kernels  52.8 us (99%)
  between operations  0.64 us (1%)
    pallas_call x1, Pallas kernels, shards(): pl.pallas_call(functools.partial(kernel, n, folded), out_shape=(jax.Shape...  49.3 us
    pallas_call x1, Pallas kernels, shards(): pl.pallas_call(functools.partial(scale_kernel, entries), grid=(grid,), ou...  3.46 us

profile of v4, /device:TPU:0, one launch (start us, length us, event | category | flops | bytes accessed | tf_op | source)
XLA Modules:
  0.0 53.5 jit_solution(3811684920730273515)
XLA Ops:
  0.6 49.3 %tail_step.1 = (f32[8,128]{1,0:T(8,128)}, f32[1024,256]{1,0:T(8,128)}, f32[1,1024]{1,0:T(1,128)}) custom-call(bf16[256,256]{1,0:T(8,128)(2,1)} %draws_ref.1, bf16[256,256]{1,0:T(8,128)(2,1)} %mix_hbm.1, bf16[1024,256]{1,0:T(8,128)(2,1)} %load_hbm.1, f32[1,1024]{1,0:T(1,128)} %bitcast.8, f32[1,1024]{1,0:T(1,128)} %bitcast.9, s32[1,1024]{1,0:T(1,128)} %bitcast.10, ...), custom_call_target="tpu_custom_call" | custom-call | tf_op jit(solution)/shard_map/tail_step/pallas_call | solution.py:451
  50.0 3.5 %scale_step.1 = (f32[1,128]{1,0:T(1,128)}, f32[1024,256]{1,0:T(8,128)}, f32[1,1024]{1,0:T(1,128)}) custom-call(f32[8,128]{1,0:T(8,128)} %get-tuple-element.9.final_ref, f32[1024,256]{1,0:T(8,128)} %get-tuple-element.10.raw_ref, f32[1,1024]{1,0:T(1,128)} %get-tuple-element.11.raw_conv_ref), custom_call_target="tpu_custom_call" | custom-call | tf_op jit(solution)/shard_map/scale_step/pallas_call | solution.py:518
